TPU v7x, 32 devices: a whole 2x2x4 slice. The times are simulated.
32 devices in a mesh: batch: 8 (over z, core), head: 4 (over y, x).
Axes of the slice: x: 2, y: 2, z: 4, core: 2. Of those that a mesh axis runs over, the one named last changes fastest.
Arguments:
- hidden_in: bfloat16 [2048, 2048], P(('batch', 'head')), may hold values from -6 to 6
- norm1_gain: float32 [2048], replicated, may hold values from 0.5 to 1.5
- qkv_weight: bfloat16 [3, 2048, 2048], P(None, None, 'head'), may hold values from -0.125 to 0.125
- beta_weight: bfloat16 [2048, 16], P(None, 'head'), may hold values from -0.125 to 0.125
- conv_weight: bfloat16 [3, 4, 2048], P(None, None, 'head'), may hold values from -3 to 3
- out_gain: float32 [128], replicated, may hold values from 0.5 to 1.5
- out_weight: bfloat16 [2048, 2048], P('head'), may hold values from -0.125 to 0.125
- norm2_gain: float32 [2048], replicated, may hold values from 0.5 to 1.5
- gate_up_weight: bfloat16 [2, 2048, 5632], P(None, None, 'head'), may hold values from -0.125 to 0.125
- down_weight: bfloat16 [5632, 2048], P('head'), may hold values from -0.078125 to 0.078125
- block_segments: int32 [8, 4], P('batch'), may hold values from 0 to 2, never falling along the last dimension, each value on 1 to 2 neighbouring positions
- cotangent: bfloat16 [2048, 2048], P(('batch', 'head')), may hold values from -6 to 6
Outputs:
- block_out: bfloat16 [2048, 2048], P(('batch', 'head'))
- input_grad: float32 [2048, 2048], P(('batch', 'head'))
- norm1_gain_grad: float32 [2048], replicated
- qkv_grad: float32 [3, 2048, 2048], P(None, None, 'head')
- beta_grad: float32 [2048, 16], P(None, 'head')
- conv_grad: float32 [3, 4, 2048], P(None, None, 'head')
- out_gain_grad: float32 [128], replicated
- out_grad: float32 [2048, 2048], P('head')
- norm2_gain_grad: float32 [2048], replicated
- gate_up_grad: float32 [2, 2048, 5632], P(None, None, 'head')
- down_grad: float32 [5632, 2048], P('head')
Inputs may be any that keep to these rules, and one draw needn't show every extreme that they name: `block_segments`: each row gives, for each block of 64 tokens of one group in order, the number of the sequence it belongs to: three sequences in every group, numbered from 0 and never falling; each covers 1 to 2 blocks and one covers exactly 2.
All inputs are finite; a program needn't handle non-finite values.
Results may differ from a plain program's by a relative error of at most 0.02.
Values may be sent and summed in bfloat16 or wider, within the bound.
No kernel may reach another device: no remote copies, remote signals or barrier semaphores. Data moves between devices by JAX's collectives and lax.ppermute only.
A program may use at most 256 MiB of HBM per device.

v0:
```python
import jax
import jax.numpy as jnp
from jax import lax
from jax.sharding import PartitionSpec as P

highest_precision = lax.Precision.HIGHEST


def rms_norm(values, gain, epsilon):
    return values * lax.rsqrt(jnp.mean(values * values, axis=-1, keepdims=True) + epsilon) * gain


def unit_rows(field):
    return field * lax.rsqrt(jnp.sum(field * field, axis=-1, keepdims=True) + 1e-06)


def conv_masks(token_segments, taps):
    masks = []
    for shift in range(1, taps):
        earlier = jnp.concatenate([jnp.full((shift,), -1, jnp.int32), token_segments[:-shift]])
        masks.append((earlier == token_segments).astype(jnp.float32)[:, None])
    return masks


def short_conv(values, taps, masks):
    result = values * taps[0]
    for shift in range(1, taps.shape[0]):
        moved = jnp.concatenate(
            [jnp.zeros((shift, values.shape[1]), jnp.float32), values[:-shift]], axis=0
        )
        result = result + moved * taps[shift] * masks[shift - 1]
    return result


def block_step(running_state, inputs):
    query_rows, key, value, beta, keep = inputs
    running_state = running_state * keep
    length = key.shape[1]
    strict = jnp.tril(jnp.ones((length, length), jnp.float32), -1)
    inclusive = jnp.tril(jnp.ones((length, length), jnp.float32))
    keyed = (
        jnp.einsum("hck,hdk->hcd", key * beta[:, :, None], key, precision=highest_precision)
        * strict
    )
    power = -keyed
    inverse = jnp.eye(length, dtype=jnp.float32) + power
    for level in range(length.bit_length() - 2):
        power = jnp.einsum("hcd,hde->hce", power, power, precision=highest_precision)
        inverse = inverse + jnp.einsum("hcd,hde->hce", inverse, power, precision=highest_precision)
    weights = inverse * beta[:, None, :]
    weighted_key = jnp.einsum("hcd,hdk->hck", weights, key, precision=highest_precision)
    weighted_value = jnp.einsum("kzw,kwp->kzp", weights, value, precision=highest_precision)
    fresh_values = weighted_value - jnp.einsum(
        "imd,ide->ime", weighted_key, running_state, precision=highest_precision
    )
    score_matrix = (
        jnp.einsum("hck,hdk->hcd", query_rows, key, precision=highest_precision) * inclusive
    )
    output_rows = jnp.einsum(
        "imd,ide->ime", query_rows, running_state, precision=highest_precision
    ) + jnp.einsum("kzw,kwp->kzp", score_matrix, fresh_values, precision=highest_precision)
    running_state = running_state + jnp.einsum(
        "sbi,sbw->siw", key, fresh_values, precision=highest_precision
    )
    return (running_state, output_rows)


def local_mixer(projected, beta_logit, conv_taps, gain, token_segments, keep):
    masks = conv_masks(token_segments, conv_taps.shape[1])
    heads = beta_logit.shape[1]
    length = projected.shape[1]
    width = projected.shape[2] // heads
    blocks = keep.shape[0]
    size = length // blocks
    parts = []
    for which in range(3):
        convolved = jax.nn.silu(short_conv(projected[which], conv_taps[which], masks))
        parts.append(convolved.reshape(length, heads, width))
    query_rows = unit_rows(parts[0]) * width ** (-0.5)
    key = unit_rows(parts[1])
    value = parts[2]
    beta = jax.nn.sigmoid(beta_logit)

    def arrange(field):
        return field.reshape(blocks, size, heads, width).transpose(0, 2, 1, 3)

    beta_blocks = beta.reshape(blocks, size, heads).transpose(0, 2, 1)
    initial = jnp.zeros((heads, width, width), jnp.float32)
    final, outputs = lax.scan(
        jax.checkpoint(block_step),
        initial,
        (arrange(query_rows), arrange(key), arrange(value), beta_blocks, keep),
    )
    outputs = outputs.transpose(0, 2, 1, 3).reshape(length, heads, width)
    return rms_norm(outputs, gain, 1e-05).reshape(length, heads * width)


def norm_rows(values, gain):
    return rms_norm(values, gain, 1e-06)


def per_device(
    hidden_in,
    norm1_gain,
    qkv_weight,
    beta_weight,
    conv_weight,
    out_gain,
    out_weight,
    norm2_gain,
    gate_up_weight,
    down_weight,
    block_segments,
    cotangent,
):
    segments = block_segments[0]
    blocks = segments.shape[0]
    rows_in = hidden_in.astype(jnp.float32)
    normed_one, first_pull = jax.vjp(norm_rows, rows_in, norm1_gain)
    normed_low = normed_one.astype(jnp.bfloat16)
    normed_all = lax.all_gather(normed_low, "head", axis=0, tiled=True)
    length = normed_all.shape[0]
    token_segments = jnp.repeat(segments, length // blocks)
    keep = jnp.concatenate(
        [jnp.zeros((1,), jnp.float32), (segments[1:] == segments[:-1]).astype(jnp.float32)]
    )
    projected = jnp.einsum(
        "td,sde->ste", normed_all, qkv_weight, preferred_element_type=jnp.float32
    )
    beta_logit = jnp.dot(normed_all, beta_weight, preferred_element_type=jnp.float32)

    def mixer(projected_in, beta_in, conv_in, gain_in):
        return local_mixer(projected_in, beta_in, conv_in, gain_in, token_segments, keep)

    mixer_out, mixer_pull = jax.vjp(
        mixer, projected, beta_logit, conv_weight.astype(jnp.float32), out_gain
    )
    mixer_low = mixer_out.astype(jnp.bfloat16)
    piece = mixer_low
    attn_rows = lax.psum_scatter(
        jnp.dot(piece, out_weight, preferred_element_type=jnp.float32).astype(jnp.bfloat16),
        "head",
        scatter_dimension=0,
        tiled=True,
    ).astype(jnp.float32)
    middle = rows_in + attn_rows
    normed_two, second_pull = jax.vjp(norm_rows, middle, norm2_gain)
    second_low = normed_two.astype(jnp.bfloat16)
    second_all = lax.all_gather(second_low, "head", axis=0, tiled=True)
    gate_up = jnp.einsum(
        "td,sdf->stf", second_all, gate_up_weight, preferred_element_type=jnp.float32
    )
    sigmoid_gate = jax.nn.sigmoid(gate_up[0])
    silu_gate = gate_up[0] * sigmoid_gate
    hidden_low = (silu_gate * gate_up[1]).astype(jnp.bfloat16)
    piece = hidden_low
    ffn_rows = lax.psum_scatter(
        jnp.dot(piece, down_weight, preferred_element_type=jnp.float32).astype(jnp.bfloat16),
        "head",
        scatter_dimension=0,
        tiled=True,
    ).astype(jnp.float32)
    block_out = (middle + ffn_rows).astype(jnp.bfloat16)
    cot_all = lax.all_gather(cotangent, "head", axis=0, tiled=True)
    down_grad = jnp.einsum("tf,td->fd", hidden_low, cot_all, preferred_element_type=jnp.float32)
    hidden_grad = jnp.einsum("td,fd->tf", cot_all, down_weight, preferred_element_type=jnp.float32)
    gate_grad = hidden_grad * gate_up[1] * sigmoid_gate * (1.0 + gate_up[0] * (1.0 - sigmoid_gate))
    up_grad = hidden_grad * silu_gate
    gate_up_low = jnp.stack([gate_grad, up_grad]).astype(jnp.bfloat16)
    gate_up_grad = jnp.einsum(
        "td,stf->sdf", second_all, gate_up_low, preferred_element_type=jnp.float32
    )
    piece = gate_up_low
    second_grad = lax.psum_scatter(
        jnp.einsum("stf,sdf->td", piece, gate_up_weight, preferred_element_type=jnp.float32).astype(
            jnp.bfloat16
        ),
        "head",
        scatter_dimension=0,
        tiled=True,
    ).astype(jnp.float32)
    middle_part, norm2_gain_grad = second_pull(second_grad)
    middle_grad = cotangent.astype(jnp.float32) + middle_part
    mixer_grad_all = lax.all_gather(middle_grad.astype(jnp.bfloat16), "head", axis=0, tiled=True)
    out_grad = jnp.einsum(
        "tc,td->cd", mixer_low, mixer_grad_all, preferred_element_type=jnp.float32
    )
    mixer_in_grad = jnp.einsum(
        "td,cd->tc", mixer_grad_all, out_weight, preferred_element_type=jnp.float32
    )
    projected_grad, beta_logit_grad, conv_grad, out_gain_grad = mixer_pull(mixer_in_grad)
    projected_low = projected_grad.astype(jnp.bfloat16)
    beta_low = beta_logit_grad.astype(jnp.bfloat16)
    qkv_grad = jnp.einsum(
        "td,ste->sde", normed_all, projected_low, preferred_element_type=jnp.float32
    )
    beta_grad = jnp.einsum("td,th->dh", normed_all, beta_low, preferred_element_type=jnp.float32)
    piece = projected_low
    first_grad = lax.psum_scatter(
        (
            jnp.einsum("ste,sde->td", piece, qkv_weight, preferred_element_type=jnp.float32)
            + jnp.einsum("th,dh->td", beta_low, beta_weight, preferred_element_type=jnp.float32)
        ).astype(jnp.bfloat16),
        "head",
        scatter_dimension=0,
        tiled=True,
    ).astype(jnp.float32)
    rows_part, norm1_gain_grad = first_pull(first_grad)
    input_grad = middle_grad + rows_part
    norm1_gain_grad, norm2_gain_grad, out_gain_grad = lax.psum(
        (norm1_gain_grad, norm2_gain_grad, out_gain_grad), ("batch", "head")
    )
    qkv_grad, beta_grad, conv_grad, out_grad, gate_up_grad, down_grad = (
        lax.psum(qkv_grad.astype(jnp.bfloat16), "batch").astype(jnp.float32),
        lax.psum(beta_grad.astype(jnp.bfloat16), "batch").astype(jnp.float32),
        lax.psum(conv_grad.astype(jnp.bfloat16), "batch").astype(jnp.float32),
        lax.psum(out_grad.astype(jnp.bfloat16), "batch").astype(jnp.float32),
        lax.psum(gate_up_grad.astype(jnp.bfloat16), "batch").astype(jnp.float32),
        lax.psum(down_grad.astype(jnp.bfloat16), "batch").astype(jnp.float32),
    )
    return (
        block_out,
        input_grad,
        norm1_gain_grad,
        qkv_grad,
        beta_grad,
        conv_grad,
        out_gain_grad,
        out_grad,
        norm2_gain_grad,
        gate_up_grad,
        down_grad,
    )


def solution(mesh):
    placed = (
        P(("batch", "head"), None),
        P(),
        P(None, None, "head"),
        P(None, "head"),
        P(None, None, "head"),
        P(),
        P("head", None),
        P(),
        P(None, None, "head"),
        P("head", None),
        P("batch", None),
        P(("batch", "head"), None),
    )
    return jax.shard_map(
        per_device,
        mesh=mesh,
        in_specs=placed,
        out_specs=(
            P(("batch", "head"), None),
            P(("batch", "head"), None),
            P(),
            P(None, None, "head"),
            P(None, "head"),
            P(None, None, "head"),
            P(),
            P("head", None),
            P(),
            P(None, None, "head"),
            P("head", None),
        ),
        check_vma=False,
    )
```

profile of v0, /device:TPU:0, one launch (start us, length us, event | category | flops | bytes accessed | tf_op | source)
XLA Modules:
  0.0 1058.0 jit_solution(14581154062135182777)
XLA Ops:
  9.7 1.8 fusion.112
  16.7 24.1 %all-gather.5.cloned.1.call-done = bf16[256,2048]{1,0:T(8,128)(2,1)} async-done(((bf16[64,2048]{1,0:T(8,128)(2,1)}), bf16[256,2048]{1,0:T(8,128)(2,1)}) %all-gather.5.cloned.1.call-update) | async-done | bytes 1048592 | tf_op jit(solution)/shard_map/all_gather | solution.py:121
  40.8 4.9 convolution_bitcast_fusion.4
  47.4 1.9 fusion.144
  51.1 2.0 reshape.449
  53.1 2.0 reshape.448
  55.2 2.4 fusion.143
  64.4 2.0 reshape.447
  70.9 2.2 copy_bitcast_fusion
  73.9 54.5 %while.38 = (s32[]{:T(128)}, f32[4,128,128]{2,1,0:T(8,128)S(1)}, f32[4,4,64,128]{3,2,1,0:T(8,128)}, f32[4,4,128,128]{3,2,1,0:T(8,128)}, f32[4]{0:T(128)}, /*inde...) while((s32[]{:T(128)}, f32[4,128,128]{2,1,0:T(8,128)S(1)}, ...), condition=%wide.region_4.5_spmd.clone, body=%wide.region_3.4_spmd.clone.sunk | while | flops 403464192 | bytes 6104994 | solution.py:89
  83.0 2.6 fusion.526
  96.6 2.6 fusion.526
  110.2 2.6 fusion.526
  123.9 2.6 fusion.526
  133.2 1.7 convolution_convert_fusion.2
  135.0 28.0 %reduce-scatter.5.cloned.1.call-done = bf16[64,2048]{1,0:T(8,128)(2,1)} async-done(((bf16[256,2048]{1,0:T(8,128)(2,1)}), bf16[64,2048]{1,0:T(8,128)(2,1)}) %reduce-scatter.5.cloned.1.call-update) | async-done | bytes 262160 | tf_op jit(solution)/shard_map/reduce_scatter | solution.py:140
  164.2 1.8 multiply_convert_fusion.3
  166.8 25.9 %all-gather.7.cloned.1.call-done = bf16[256,2048]{1,0:T(8,128)(2,1)} async-done(((bf16[64,2048]{1,0:T(8,128)(2,1)}), bf16[256,2048]{1,0:T(8,128)(2,1)}) %all-gather.7.cloned.1.call-update) | async-done | bytes 1048592 | tf_op jit(solution)/shard_map/all_gather | solution.py:149
  192.7 9.3 convolution_bitcast_fusion.1
  202.0 18.9 %all-gather.9.cloned.1.call-done = bf16[256,2048]{1,0:T(8,128)(2,1)} async-done(((bf16[64,2048]{1,0:T(8,128)(2,1)}), bf16[256,2048]{1,0:T(8,128)(2,1)}) %all-gather.9.cloned.1.call-update) | async-done | bytes 1048592 | tf_op jit(solution)/shard_map/all_gather | solution.py:164
  220.9 6.9 fusion.107
  228.9 8.5 fusion.96
  237.5 28.0 %reduce-scatter.9.cloned.1.call-done = bf16[64,2048]{1,0:T(8,128)(2,1)} async-done(((bf16[256,2048]{1,0:T(8,128)(2,1)}), bf16[64,2048]{1,0:T(8,128)(2,1)}) %reduce-scatter.9.cloned.1.call-update) | async-done | bytes 262160 | tf_op jit(solution)/shard_map/reduce_scatter | solution.py:174
  265.5 1.8 fusion.114
  267.3 1.9 fusion.142
  269.5 26.4 %all-gather.11.cloned.1.call-done = bf16[256,2048]{1,0:T(8,128)(2,1)} async-done(((bf16[64,2048]{1,0:T(8,128)(2,1)}), bf16[256,2048]{1,0:T(8,128)(2,1)}) %all-gather.11.cloned.1.call-update) | async-done | bytes 1048592 | tf_op jit(solution)/shard_map/all_gather | solution.py:184
  295.9 3.1 multiply_reduce_fusion.2
  304.0 119.5 %while.39 = (s32[]{:T(128)}, f32[4,128,128]{2,1,0:T(8,128)}, f32[4,4,64,128]{3,2,1,0:T(8,128)S(1)}, f32[4,4,64,128]{3,2,1,0:T(8,128)}, f32[4,4,64,128]{3,2,1,0:T...) while((s32[]{:T(128)}, f32[4,128,128]{2,1,0:T(8,128)}, ...), condition=%wide.region_15.16_spmd.clone, body=%wide.region_12.15_spmd.clone.sunk | while | flops 1083678464 | bytes 18188008 | solution.py:89
  331.3 1.9 fusion.643
  361.2 1.9 fusion.643
  391.2 1.9 fusion.643
  421.2 1.9 fusion.643
  439.1 2.9 multiply_reduce_fusion.11
  442.1 5.2 convolution_bitcast_fusion.2
  447.3 1.5 fusion.97
  448.9 5.5 convolution_convert_fusion.3
  454.5 4.2 convolution_convert_fusion
  458.7 6.4 convert_bitcast_fusion.1
  465.2 2.1 convolution_convert_fusion.1
  467.3 4.6 convert_bitcast_fusion.2
  472.2 28.4 %all-reduce.39 = (bf16[2048,4]{0,1:T(4,128)(2,1)S(1)}, bf16[3,4,512]{2,1,0:T(4,128)(2,1)S(1)}) all-reduce(bf16[2048,4]{0,1:T(4,128)(2,1)S(1)} %convolution_convert_fusion.4, bf16[3,4,512]{2,1,0:T(4,128)(2,1)S(1)} %add_convert_fusion.2), channel_id=1, replica_groups=mesh['batch'=8,'head'=4] {'batch'}, use_global_device_ids=true, to_apply=%region_23.24 | all-reduce | flops 14336 | bytes 57344 | tf_op jit(solution)/shard_map/psum | solution.py:215
  503.2 38.7 %all-reduce.38 = (f32[2048]{0:T(1024)}, f32[128]{0:T(128)}, f32[2048]{0:T(1024)}) all-reduce(f32[2048]{0:T(1024)S(1)} %get-tuple-element.622, f32[128]{0:T(128)S(1)} %bitcast_reduce_fusion, f32[2048]{0:T(1024)S(1)} %copy-done.74), channel_id=1, replica_groups=mesh['batch'=8,'head'=4] {'batch','head'}, use_global_device_ids=true, to_apply=%region_21.22 | all-reduce | flops 4224 | bytes 33792 | tf_op jit(solution)/shard_map/psum | solution.py:210
  541.9 2.3 fusion.124
  544.3 469.3 %all-reduce.43.cloned.1.call-done = (bf16[3,2048,512]{1,2,0:T(8,128)(2,1)}, bf16[2,2048,1408]{1,2,0:T(8,128)(2,1)}, bf16[512,2048]{1,0:T(8,128)(2,1)}, bf16[1408,2048]{1,0:T(8,128)(2,1)}) async-done(((bf16[3,2048,512]{1,2,0:T(8,128)(2,1)}, bf16[2,2048,1408]{1,2,0:T(8,128)(2,1)}, bf16[512,2048]{1,0:T(8,128)(2,1)}, bf16[1408,2048]{1,0:T(8,128)(2,1)}), (bf16[3,2048,512]{1,2,0:T(8,128)(2,1)}, ...) | async-done | bytes 25690128 | tf_op jit(solution)/shard_map/psum | solution.py:214
  1013.5 17.0 %copy.272 = f32[2,2048,1408]{2,1,0:T(8,128)} copy(bf16[2,2048,1408]{1,2,0:T(8,128)(2,1)} %get-tuple-element.676) | data formatting | bytes 34603008
  1030.5 9.4 copy.271
  1039.9 8.8 convert_element_type.177
  1048.8 2.5 convert_element_type.172
  (683 shorter events, 207.6 us)
Async XLA Ops:
  7.2 126.1 %copy-start = (bf16[512,2048]{1,0:T(8,128)(2,1)S(1)}, bf16[512,2048]{1,0:T(8,128)(2,1)}, u32[]{:S(2)}) copy-start(bf16[512,2048]{1,0:T(8,128)(2,1)} %param.22) | copy-start | bytes 6291460
  7.2 33.6 %all-gather.5.cloned.1.call-start = ((), (), s32[]{:S(2)}) async-start(), calls=%async_computation.4 | async-start | bytes 1310720 | tf_op jit(solution)/shard_map/all_gather | solution.py:121
  11.5 151.6 %reduce-scatter.5.cloned.1.call-start = ((), (), s32[]{:S(2)}) async-start(), calls=%async_computation.5 | async-start | bytes 1310720 | tf_op jit(solution)/shard_map/reduce_scatter | solution.py:140
  15.7 39.5 %copy-start.100 = (f32[256]{0:T(256)}, f32[256]{0:T(256)S(1)}, u32[]{:S(2)}) copy-start(f32[256]{0:T(256)S(1)} %get-tuple-element.767) | copy-start | bytes 3076
  15.7 39.5 %copy-start.102 = (f32[256]{0:T(256)}, f32[256]{0:T(256)S(1)}, u32[]{:S(2)}) copy-start(f32[256]{0:T(256)S(1)} %get-tuple-element.769) | copy-start | bytes 3076
  15.7 39.5 %copy-start.104 = (f32[256]{0:T(256)}, f32[256]{0:T(256)S(1)}, u32[]{:S(2)}) copy-start(f32[256]{0:T(256)S(1)} %get-tuple-element.768) | copy-start | bytes 3076
  16.6 30.4 %copy-start.76 = (f32[1,1,512]{2,1,0:T(1,128)}, f32[1,1,512]{2,1,0:T(1,128)S(1)}, u32[]{:S(2)}) copy-start(f32[1,1,512]{2,1,0:T(1,128)S(1)} %get-tuple-element.739) | copy-start | bytes 6148
  16.6 30.4 %copy-start.78 = (f32[1,1,512]{2,1,0:T(1,128)}, f32[1,1,512]{2,1,0:T(1,128)S(1)}, u32[]{:S(2)}) copy-start(f32[1,1,512]{2,1,0:T(1,128)S(1)} %get-tuple-element.743) | copy-start | bytes 6148
  16.6 30.4 %copy-start.80 = (f32[1,1,512]{2,1,0:T(1,128)}, f32[1,1,512]{2,1,0:T(1,128)S(1)}, u32[]{:S(2)}) copy-start(f32[1,1,512]{2,1,0:T(1,128)S(1)} %get-tuple-element.746) | copy-start | bytes 6148
  16.6 30.4 %copy-start.82 = (f32[1,1,512]{2,1,0:T(1,128)}, f32[1,1,512]{2,1,0:T(1,128)S(1)}, u32[]{:S(2)}) copy-start(f32[1,1,512]{2,1,0:T(1,128)S(1)} %get-tuple-element.742) | copy-start | bytes 6148
  16.6 30.4 %copy-start.84 = (f32[1,1,512]{2,1,0:T(1,128)}, f32[1,1,512]{2,1,0:T(1,128)S(1)}, u32[]{:S(2)}) copy-start(f32[1,1,512]{2,1,0:T(1,128)S(1)} %get-tuple-element.745) | copy-start | bytes 6148
  16.6 30.4 %copy-start.86 = (f32[1,1,512]{2,1,0:T(1,128)}, f32[1,1,512]{2,1,0:T(1,128)S(1)}, u32[]{:S(2)}) copy-start(f32[1,1,512]{2,1,0:T(1,128)S(1)} %get-tuple-element.744) | copy-start | bytes 6148
  16.6 30.4 %copy-start.88 = (f32[1,1,512]{2,1,0:T(1,128)}, f32[1,1,512]{2,1,0:T(1,128)S(1)}, u32[]{:S(2)}) copy-start(f32[1,1,512]{2,1,0:T(1,128)S(1)} %get-tuple-element.741) | copy-start | bytes 6148
  16.7 30.4 %copy-start.90 = (f32[1,1,512]{2,1,0:T(1,128)}, f32[1,1,512]{2,1,0:T(1,128)S(1)}, u32[]{:S(2)}) copy-start(f32[1,1,512]{2,1,0:T(1,128)S(1)} %get-tuple-element.740) | copy-start | bytes 6148
  16.7 38.5 %copy-start.92 = (f32[1,1,512]{2,1,0:T(1,128)}, f32[1,1,512]{2,1,0:T(1,128)S(1)}, u32[]{:S(2)}) copy-start(f32[1,1,512]{2,1,0:T(1,128)S(1)} %get-tuple-element.747) | copy-start | bytes 6148
  16.7 38.5 %copy-start.94 = (f32[1,1,512]{2,1,0:T(1,128)}, f32[1,1,512]{2,1,0:T(1,128)S(1)}, u32[]{:S(2)}) copy-start(f32[1,1,512]{2,1,0:T(1,128)S(1)} %get-tuple-element.750) | copy-start | bytes 6148
  16.7 38.5 %copy-start.96 = (f32[1,1,512]{2,1,0:T(1,128)}, f32[1,1,512]{2,1,0:T(1,128)S(1)}, u32[]{:S(2)}) copy-start(f32[1,1,512]{2,1,0:T(1,128)S(1)} %get-tuple-element.748) | copy-start | bytes 6148
  16.7 38.5 %copy-start.98 = (f32[1,1,512]{2,1,0:T(1,128)}, f32[1,1,512]{2,1,0:T(1,128)S(1)}, u32[]{:S(2)}) copy-start(f32[1,1,512]{2,1,0:T(1,128)S(1)} %get-tuple-element.749) | copy-start | bytes 6148
  45.9 9.3 copy-start.17
  46.1 9.1 copy-start.23
  60.9 8.9 copy-start.6
  60.9 8.9 copy-start.66
  133.2 29.8 %copy-start.4 = (bf16[64,2048]{1,0:T(8,128)(2,1)S(1)}, bf16[64,2048]{1,0:T(8,128)(2,1)}, u32[]{:S(2)}) copy-start(bf16[64,2048]{1,0:T(8,128)(2,1)} %param.16) | copy-start | bytes 786436
  133.2 30.9 %copy-start.60 = (f32[2048]{0:T(1024)S(1)}, f32[2048]{0:T(1024)}, u32[]{:S(2)}) copy-start(f32[2048]{0:T(1024)} %param.23) | copy-start | bytes 24580
  135.0 57.7 %all-gather.7.cloned.1.call-start = ((), (), s32[]{:S(2)}) async-start(), calls=%async_computation.6 | async-start | bytes 1310720 | tf_op jit(solution)/shard_map/all_gather | solution.py:149
  164.2 103.1 %copy-start.108 = (f32[64]{0:T(128)}, f32[64]{0:T(128)S(1)}, u32[]{:S(2)}) copy-start(f32[64]{0:T(128)S(1)} %fusion.139) | copy-start | bytes 772
  166.0 54.9 %all-gather.9.cloned.1.call-start = ((), (), s32[]{:S(2)}) async-start(), calls=%async_computation.8 | async-start | bytes 1310720 | tf_op jit(solution)/shard_map/all_gather | solution.py:164
  166.6 98.9 %reduce-scatter.9.cloned.1.call-start = ((), (), s32[]{:S(2)}) async-start(), calls=%async_computation.9 | async-start | bytes 1310720 | tf_op jit(solution)/shard_map/reduce_scatter | solution.py:174
  228.9 36.6 %copy-start.8 = (bf16[64,2048]{1,0:T(8,128)(2,1)S(1)}, bf16[64,2048]{1,0:T(8,128)(2,1)}, u32[]{:S(2)}) copy-start(bf16[64,2048]{1,0:T(8,128)(2,1)} %reduce-scatter.5.cloned.1.call-done) | copy-start | bytes 786436
  228.9 38.4 %copy-start.40 = (bf16[64,2048]{1,0:T(8,128)(2,1)S(1)}, bf16[64,2048]{1,0:T(8,128)(2,1)}, u32[]{:S(2)}) copy-start(bf16[64,2048]{1,0:T(8,128)(2,1)} %param.27) | copy-start | bytes 786436
  237.4 31.9 %copy-start.72 = (f32[256,4]{0,1:T(4,128)S(1)}, f32[256,4]{0,1:T(4,128)}, u32[]{:S(2)}) copy-start(f32[256,4]{0,1:T(4,128)} %copy-done.71) | copy-start | bytes 12292
  237.4 58.4 %all-gather.11.cloned.1.call-start = ((), (), s32[]{:S(2)}) async-start(), calls=%async_computation.10 | async-start | bytes 1310720 | tf_op jit(solution)/shard_map/all_gather | solution.py:184
  269.2 232.7 %reduce-scatter.11.cloned.1.call-start = ((), (), s32[]{:S(2)}) async-start(), calls=%async_computation.11 | async-start | bytes 1310720 | tf_op jit(solution)/shard_map/reduce_scatter | solution.py:199
  269.4 30.7 %copy-start.5 = (f32[4,4,64,128]{3,2,1,0:T(8,128)S(1)}, f32[4,4,64,128]{3,2,1,0:T(8,128)}, u32[]{:S(2)}) copy-start(f32[4,4,64,128]{3,2,1,0:T(8,128)} %get-tuple-element.340) | copy-start | bytes 1572868
  269.5 30.7 %copy-start.110 = (f32[128]{0:T(128)S(1)}, f32[128]{0:T(128)}, u32[]{:S(2)}) copy-start(f32[128]{0:T(128)} %param.21) | copy-start | bytes 1540
  448.8 93.1 %reduce-scatter.7.cloned.1.call-start = ((), (), s32[]{:S(2)}) async-start(), calls=%async_computation.7 | async-start | bytes 1310720 | tf_op jit(solution)/shard_map/reduce_scatter | solution.py:157
  454.4 559.1 %all-reduce.43.cloned.1.call-start = ((), (), s32[]{:S(2)}) async-start(), calls=%async_computation.12 | async-start | bytes 51380224 | tf_op jit(solution)/shard_map/psum | solution.py:214
  458.7 6.4 copy-start.37
  471.8 30.1 %copy-start.61 = (f32[2048]{0:T(1024)S(1)}, f32[2048]{0:T(1024)}, u32[]{:S(2)}) copy-start(f32[2048]{0:T(1024)} %param.17) | copy-start | bytes 24580
  471.8 30.1 %copy-start.112 = (f32[64]{0:T(128)S(1)}, f32[64]{0:T(128)}, u32[]{:S(2)}) copy-start(f32[64]{0:T(128)} %copy-done.111) | copy-start | bytes 772
  471.8 31.4 %copy-start.74 = (f32[2048]{0:T(1024)S(1)}, f32[2048]{0:T(1024)}, u32[]{:S(2)}) copy-start(f32[2048]{0:T(1024)} %get-tuple-element.620) | copy-start | bytes 24580
  471.8 70.0 %copy-start.116 = (f32[64]{0:T(128)S(1)}, f32[64]{0:T(128)}, u32[]{:S(2)}) copy-start(f32[64]{0:T(128)} %copy-done.115) | copy-start | bytes 772
  471.8 70.1 %copy-start.9 = (bf16[64,2048]{1,0:T(8,128)(2,1)S(1)}, bf16[64,2048]{1,0:T(8,128)(2,1)}, u32[]{:S(2)}) copy-start(bf16[64,2048]{1,0:T(8,128)(2,1)} %reduce-scatter.5.cloned.1.call-done) | copy-start | bytes 786436
  471.8 70.1 %copy-start.41 = (bf16[64,2048]{1,0:T(8,128)(2,1)S(1)}, bf16[64,2048]{1,0:T(8,128)(2,1)}, u32[]{:S(2)}) copy-start(bf16[64,2048]{1,0:T(8,128)(2,1)} %param.27) | copy-start | bytes 786436
  471.9 70.1 %copy-start.42 = (bf16[64,2048]{1,0:T(8,128)(2,1)S(1)}, bf16[64,2048]{1,0:T(8,128)(2,1)}, u32[]{:S(2)}) copy-start(bf16[64,2048]{1,0:T(8,128)(2,1)} %reduce-scatter.9.cloned.1.call-done) | copy-start | bytes 786436
  471.9 70.1 %copy-start.109 = (f32[64]{0:T(128)S(1)}, f32[64]{0:T(128)}, u32[]{:S(2)}) copy-start(f32[64]{0:T(128)} %copy-done.108) | copy-start | bytes 772
  471.9 70.1 %copy-start.114 = (f32[64]{0:T(128)S(1)}, f32[64]{0:T(128)}, u32[]{:S(2)}) copy-start(f32[64]{0:T(128)} %copy-done.113) | copy-start | bytes 772
  1039.9 8.8 copy-start.43
  (78 other events, 192.4 us)
Sparse Core Ops, SparseCore 0:
  11.6 29.2 all-gather.4
  135.1 27.9 reduce-scatter.4
  166.1 26.4 all-gather.6
  194.4 26.4 all-gather.8
  237.5 27.9 reduce-scatter.8
  269.3 26.4 all-gather.10
  448.9 27.9 reduce-scatter.10
  479.8 27.9 reduce-scatter.6
  511.8 501.6 all-reduce.42
where the time goes:
time: 1070 us; the launch traced here: 1060 us
  waiting for transfers between devices  621 us (58%)
  matrix products  200 us (19%)
  local copies, waits for them, and re-layouts  85.4 us (8%)
  blocking collectives  67 us (6%)
  other arithmetic  65.9 us (6%)
  between operations  15.5 us (1%)
    psum x1, waiting for transfers between devices, per_device(): lax.psum(qkv_grad.astype(jnp.bfloat16), 'batch').astype(jnp.float32)  469 us
    psum x1, blocking collectives, per_device(): lax.psum((norm1_gain_grad, norm2_gain_grad, out_gain_grad), ('batch', 'he...  38.7 us
    unnamed x237, local copies, waits for them, and re-layouts  34.6 us
    psum x1, blocking collectives, per_device(): lax.psum(beta_grad.astype(jnp.bfloat16), 'batch').astype(jnp.float32)  28.4 us
    reduce_scatter x1, waiting for transfers between devices, per_device(): lax.psum_scatter(jnp.einsum('stf,sdf->td', piece, gate_up_weight, preferr...  28 us
    reduce_scatter x1, waiting for transfers between devices, per_device(): lax.psum_scatter(jnp.dot(piece, out_weight, preferred_element_type=jnp.fl...  28 us
    all_gather x1, waiting for transfers between devices, per_device(): lax.all_gather(middle_grad.astype(jnp.bfloat16), 'head', axis=0, tiled=True)  26.4 us
    all_gather x1, waiting for transfers between devices, per_device(): second_all = lax.all_gather(second_low, 'head', axis=0, tiled=True)  25.9 us
  transfers between devices with their start and end apart: 9, of which 7 were waited for; matrix products, arithmetic and copies ran while one was open for 4% of the time, Pallas kernels for 0%

commit v1 on v0

--- a/solution.py
+++ b/solution.py
@@ -210,8 +210,9 @@
     norm1_gain_grad, norm2_gain_grad, out_gain_grad = lax.psum(
         (norm1_gain_grad, norm2_gain_grad, out_gain_grad), ("batch", "head")
     )
+    open_levels_all = lambda arr_in: jax.lax.all_gather(arr_in, "batch").sum(axis=0)
     qkv_grad, beta_grad, conv_grad, out_grad, gate_up_grad, down_grad = (
-        lax.psum(qkv_grad.astype(jnp.bfloat16), "batch").astype(jnp.float32),
+        open_levels_all(qkv_grad.astype(jnp.bfloat16)).astype(jnp.float32),
         lax.psum(beta_grad.astype(jnp.bfloat16), "batch").astype(jnp.float32),
         lax.psum(conv_grad.astype(jnp.bfloat16), "batch").astype(jnp.float32),
         lax.psum(out_grad.astype(jnp.bfloat16), "batch").astype(jnp.float32),

time: 1070 us -> 1360 us (1.27)
  waiting for transfers between devices: 621 us -> 888 us
  local copies, waits for them, and re-layouts: 85.4 us -> 101 us
  other arithmetic: 65.9 us -> 79.6 us
    all_gather x0 -> x1, waiting for transfers between devices: none -> 397 us  [per_device(): jax.lax.all_gather(arr_in, 'batch').sum(axis=0)]
    psum x1, waiting for transfers between devices: 469 us -> 339 us  [per_device(): lax.psum(gate_up_grad.astype(jnp.bfloat16), 'batch').astype(jnp.float32)]
    reduce_sum x0 -> x1, other arithmetic: none -> 20.1 us  [per_device(): jax.lax.all_gather(arr_in, 'batch').sum(axis=0)]
    unnamed x237 -> x208, local copies, waits for them, and re-layouts: 34.6 us -> 47.1 us
  transfers between devices with their start and end apart: 9 -> 10, of which waited for: 7 -> 8; matrix products, arithmetic and copies ran while one was open for 4% -> 6% of each run, Pallas kernels for 0% -> 0%
where the time goes in v1:
time: 1360 us; the launch traced here: 1350 us
  waiting for transfers between devices  888 us (65%)
  matrix products  197 us (14%)
  local copies, waits for them, and re-layouts  101 us (7%)
  other arithmetic  79.6 us (6%)
  blocking collectives  67.1 us (5%)
  between operations  15.8 us (1%)
    all_gather x1, waiting for transfers between devices, per_device(): jax.lax.all_gather(arr_in, 'batch').sum(axis=0)  397 us
    psum x1, waiting for transfers between devices, per_device(): lax.psum(gate_up_grad.astype(jnp.bfloat16), 'batch').astype(jnp.float32)  339 us
    unnamed x208, local copies, waits for them, and re-layouts  47.1 us
    psum x1, blocking collectives, per_device(): lax.psum((norm1_gain_grad, norm2_gain_grad, out_gain_grad), ('batch', 'he...  38.7 us
    psum x1, blocking collectives, per_device(): lax.psum(beta_grad.astype(jnp.bfloat16), 'batch').astype(jnp.float32)  28.4 us
    reduce_scatter x1, waiting for transfers between devices, per_device(): lax.psum_scatter(jnp.einsum('stf,sdf->td', piece, gate_up_weight, preferr...  28 us
    reduce_scatter x1, waiting for transfers between devices, per_device(): lax.psum_scatter(jnp.dot(piece, out_weight, preferred_element_type=jnp.fl...  28 us
  transfers between devices with their start and end apart: 10, of which 8 were waited for; matrix products, arithmetic and copies ran while one was open for 6% of the time, Pallas kernels for 0%

profile of v1, /device:TPU:0, one launch (start us, length us, event | category | flops | bytes accessed | tf_op | source)
XLA Modules:
  0.0 1351.5 jit_solution(6283495877814860698)
XLA Ops:
  16.5 24.2 %all-gather.7.cloned.1.call-done = bf16[256,2048]{1,0:T(8,128)(2,1)} async-done(((bf16[64,2048]{1,0:T(8,128)(2,1)}), bf16[256,2048]{1,0:T(8,128)(2,1)}) %all-gather.7.cloned.1.call-update) | async-done | bytes 1048592 | tf_op jit(solution)/shard_map/all_gather | solution.py:121
  40.7 4.9 convolution_bitcast_fusion.4
  51.3 2.0 reshape.445
  53.3 2.0 reshape.444
  55.5 3.8 fusion.144
  71.4 2.0 copy_bitcast_fusion
  73.5 46.5 %while.38 = (s32[]{:T(128)}, f32[4,128,128]{2,1,0:T(8,128)S(1)}, f32[4,4,64,128]{3,2,1,0:T(8,128)S(1)}, f32[4,4,128,128]{3,2,1,0:T(8,128)}, f32[4]{0:T(128)S(1)}...) while((s32[]{:T(128)}, f32[4,128,128]{2,1,0:T(8,128)S(1)}, ...), condition=%wide.region_4.5_spmd.clone, body=%wide.region_3.4_spmd.clone.sunk | while | flops 403464192 | bytes 6104497 | solution.py:89
  81.2 1.9 fusion.526
  92.9 1.9 fusion.526
  116.1 1.9 fusion.526
  124.5 28.0 %reduce-scatter.5.cloned.1.call-done = bf16[64,2048]{1,0:T(8,128)(2,1)} async-done(((bf16[256,2048]{1,0:T(8,128)(2,1)}), bf16[64,2048]{1,0:T(8,128)(2,1)}) %reduce-scatter.5.cloned.1.call-update) | async-done | bytes 262160 | tf_op jit(solution)/shard_map/reduce_scatter | solution.py:140
  156.3 25.9 %all-gather.9.cloned.1.call-done = bf16[256,2048]{1,0:T(8,128)(2,1)} async-done(((bf16[64,2048]{1,0:T(8,128)(2,1)}), bf16[256,2048]{1,0:T(8,128)(2,1)}) %all-gather.9.cloned.1.call-update) | async-done | bytes 1048592 | tf_op jit(solution)/shard_map/all_gather | solution.py:149
  182.1 9.3 convolution_bitcast_fusion.1
  191.5 18.9 %all-gather.11.cloned.1.call-done = bf16[256,2048]{1,0:T(8,128)(2,1)} async-done(((bf16[64,2048]{1,0:T(8,128)(2,1)}), bf16[256,2048]{1,0:T(8,128)(2,1)}) %all-gather.11.cloned.1.call-update) | async-done | bytes 1048592 | tf_op jit(solution)/shard_map/all_gather | solution.py:164
  210.4 6.9 fusion.107
  218.4 8.4 fusion.96
  226.9 28.0 %reduce-scatter.9.cloned.1.call-done = bf16[64,2048]{1,0:T(8,128)(2,1)} async-done(((bf16[256,2048]{1,0:T(8,128)(2,1)}), bf16[64,2048]{1,0:T(8,128)(2,1)}) %reduce-scatter.9.cloned.1.call-update) | async-done | bytes 262160 | tf_op jit(solution)/shard_map/reduce_scatter | solution.py:174
  256.8 2.0 fusion.142
  259.7 25.8 %all-gather.13.cloned.1.call-done = bf16[256,2048]{1,0:T(8,128)(2,1)} async-done(((bf16[64,2048]{1,0:T(8,128)(2,1)}), bf16[256,2048]{1,0:T(8,128)(2,1)}) %all-gather.13.cloned.1.call-update) | async-done | bytes 1048592 | tf_op jit(solution)/shard_map/all_gather | solution.py:184
  285.5 3.6 multiply_reduce_fusion.2
  294.0 116.6 %while.39 = (s32[]{:T(128)}, f32[4,128,128]{2,1,0:T(8,128)}, f32[4,4,64,128]{3,2,1,0:T(8,128)}, f32[4,4,64,128]{3,2,1,0:T(8,128)S(1)}, f32[4,4,64,128]{3,2,1,0:T...) while((s32[]{:T(128)}, f32[4,128,128]{2,1,0:T(8,128)}, ...), condition=%wide.region_15.16_spmd.clone, body=%wide.region_12.15_spmd.clone.sunk | while | flops 1083678464 | bytes 22383908 | solution.py:89
  309.3 1.9 fusion.646
  311.8 2.0 fusion.643
  338.5 1.9 fusion.646
  341.0 2.0 fusion.643
  367.7 1.9 fusion.646
  370.2 2.0 fusion.643
  396.9 1.9 fusion.646
  399.5 2.0 fusion.643
  410.6 2.2 copy.261
  419.1 3.1 multiply_reduce_fusion.14
  431.0 5.7 convolution_convert_fusion.3
  436.8 5.7 convolution_convert_fusion
  442.5 6.4 convert_bitcast_fusion.1
  448.9 2.1 convolution_convert_fusion.1
  452.3 4.5 convert_bitcast_fusion.2
  456.9 8.6 copy.274
  465.9 28.4 %all-reduce.39 = (bf16[2048,4]{0,1:T(4,128)(2,1)S(1)}, bf16[3,4,512]{2,1,0:T(4,128)(2,1)S(1)}) all-reduce(bf16[2048,4]{0,1:T(4,128)(2,1)S(1)} %convolution_convert_fusion.4, bf16[3,4,512]{2,1,0:T(4,128)(2,1)S(1)} %add_convert_fusion.2), channel_id=1, replica_groups=mesh['batch'=8,'head'=4] {'batch'}, use_global_device_ids=true, to_apply=%region_23.24 | all-reduce | flops 14336 | bytes 57344 | tf_op jit(solution)/shard_map/psum | solution.py:216
  496.9 38.7 %all-reduce.38 = (f32[2048]{0:T(1024)}, f32[128]{0:T(128)}, f32[2048]{0:T(1024)}) all-reduce(f32[2048]{0:T(1024)S(1)} %get-tuple-element.622, f32[128]{0:T(128)S(1)} %bitcast_reduce_fusion, f32[2048]{0:T(1024)S(1)} %copy-done.58), channel_id=1, replica_groups=mesh['batch'=8,'head'=4] {'batch','head'}, use_global_device_ids=true, to_apply=%region_21.22 | all-reduce | flops 4224 | bytes 33792 | tf_op jit(solution)/shard_map/psum | solution.py:210
  535.7 2.3 fusion.124
  538.0 339.1 %all-reduce.43.cloned.1.call-done = (bf16[2,2048,1408]{1,2,0:T(8,128)(2,1)}, bf16[512,2048]{1,0:T(8,128)(2,1)}, bf16[1408,2048]{1,0:T(8,128)(2,1)}) async-done(((bf16[2,2048,1408]{1,2,0:T(8,128)(2,1)}, bf16[512,2048]{1,0:T(8,128)(2,1)}, bf16[1408,2048]{1,0:T(8,128)(2,1)}), (bf16[2,2048,1408]{1,2,0:T(8,128)(2,1)}, bf16[512,2048]{1,0:T(8,128)(2,1)}, ...) | async-done | bytes 19398672 | tf_op jit(solution)/shard_map/psum | solution.py:219
  877.0 4.1 convert_element_type.174
  881.2 17.9 %copy.278 = f32[2,2048,1408]{2,1,0:T(8,128)} copy(bf16[2,2048,1408]{1,2,0:T(8,128)(2,1)} %get-tuple-element.675) | data formatting | bytes 34603008
  899.1 9.7 convert_element_type.179
  908.8 397.3 %all-gather.15.cloned.1.call-done = bf16[24,2048,512]{2,1,0:T(8,128)(2,1)} async-done(((bf16[3,2048,512]{2,1,0:T(8,128)(2,1)}), bf16[24,2048,512]{2,1,0:T(8,128)(2,1)}) %all-gather.15.cloned.1.call-update) | async-done | bytes 50331664 | tf_op jit(solution)/shard_map/all_gather | solution.py:213
  1306.1 20.1 %reduce_sum.306 = bf16[3,2048,512]{2,1,0:T(8,128)(2,1)} reduce(bf16[8,3,2048,512]{3,2,1,0:T(8,128)(2,1)} %bitcast.720, bf16[]{:T(256)} %constant.146.clone.1), dimensions={0}, to_apply=%region_22.23 | reduce | flops 22020096 | bytes 56623104 | tf_op jit(solution)/shard_map/reduce_sum | solution.py:213
  1326.2 8.8 copy.301
  1334.9 9.6 copy.277
  (676 shorter events, 201.7 us)
Async XLA Ops:
  7.2 115.5 %copy-start = (bf16[512,2048]{1,0:T(8,128)(2,1)S(1)}, bf16[512,2048]{1,0:T(8,128)(2,1)}, u32[]{:S(2)}) copy-start(bf16[512,2048]{1,0:T(8,128)(2,1)} %param.22) | copy-start | bytes 6291460
  7.2 33.6 %all-gather.7.cloned.1.call-start = ((), (), s32[]{:S(2)}) async-start(), calls=%async_computation.4 | async-start | bytes 1310720 | tf_op jit(solution)/shard_map/all_gather | solution.py:121
  11.4 141.1 %reduce-scatter.5.cloned.1.call-start = ((), (), s32[]{:S(2)}) async-start(), calls=%async_computation.5 | async-start | bytes 1310720 | tf_op jit(solution)/shard_map/reduce_scatter | solution.py:140
  15.5 39.9 %copy-start.84 = (f32[256]{0:T(256)}, f32[256]{0:T(256)S(1)}, u32[]{:S(2)}) copy-start(f32[256]{0:T(256)S(1)} %get-tuple-element.766) | copy-start | bytes 3076
  15.5 39.9 %copy-start.86 = (f32[256]{0:T(256)}, f32[256]{0:T(256)S(1)}, u32[]{:S(2)}) copy-start(f32[256]{0:T(256)S(1)} %get-tuple-element.768) | copy-start | bytes 3076
  15.5 39.9 %copy-start.88 = (f32[256]{0:T(256)}, f32[256]{0:T(256)S(1)}, u32[]{:S(2)}) copy-start(f32[256]{0:T(256)S(1)} %get-tuple-element.767) | copy-start | bytes 3076
  16.4 31.9 %copy-start.76 = (f32[1,1,512]{2,1,0:T(1,128)}, f32[1,1,512]{2,1,0:T(1,128)S(1)}, u32[]{:S(2)}) copy-start(f32[1,1,512]{2,1,0:T(1,128)S(1)} %get-tuple-element.746) | copy-start | bytes 6148
  16.4 31.9 %copy-start.78 = (f32[1,1,512]{2,1,0:T(1,128)}, f32[1,1,512]{2,1,0:T(1,128)S(1)}, u32[]{:S(2)}) copy-start(f32[1,1,512]{2,1,0:T(1,128)S(1)} %get-tuple-element.749) | copy-start | bytes 6148
  16.4 31.9 %copy-start.80 = (f32[1,1,512]{2,1,0:T(1,128)}, f32[1,1,512]{2,1,0:T(1,128)S(1)}, u32[]{:S(2)}) copy-start(f32[1,1,512]{2,1,0:T(1,128)S(1)} %get-tuple-element.748) | copy-start | bytes 6148
  16.4 31.9 %copy-start.82 = (f32[1,1,512]{2,1,0:T(1,128)}, f32[1,1,512]{2,1,0:T(1,128)S(1)}, u32[]{:S(2)}) copy-start(f32[1,1,512]{2,1,0:T(1,128)S(1)} %get-tuple-element.747) | copy-start | bytes 6148
  16.5 38.9 %copy-start.60 = (f32[1,1,512]{2,1,0:T(1,128)}, f32[1,1,512]{2,1,0:T(1,128)S(1)}, u32[]{:S(2)}) copy-start(f32[1,1,512]{2,1,0:T(1,128)S(1)} %get-tuple-element.738) | copy-start | bytes 6148
  16.5 38.9 %copy-start.62 = (f32[1,1,512]{2,1,0:T(1,128)}, f32[1,1,512]{2,1,0:T(1,128)S(1)}, u32[]{:S(2)}) copy-start(f32[1,1,512]{2,1,0:T(1,128)S(1)} %get-tuple-element.742) | copy-start | bytes 6148
  16.5 38.9 %copy-start.64 = (f32[1,1,512]{2,1,0:T(1,128)}, f32[1,1,512]{2,1,0:T(1,128)S(1)}, u32[]{:S(2)}) copy-start(f32[1,1,512]{2,1,0:T(1,128)S(1)} %get-tuple-element.741) | copy-start | bytes 6148
  16.5 38.9 %copy-start.66 = (f32[1,1,512]{2,1,0:T(1,128)}, f32[1,1,512]{2,1,0:T(1,128)S(1)}, u32[]{:S(2)}) copy-start(f32[1,1,512]{2,1,0:T(1,128)S(1)} %get-tuple-element.745) | copy-start | bytes 6148
  16.5 38.9 %copy-start.68 = (f32[1,1,512]{2,1,0:T(1,128)}, f32[1,1,512]{2,1,0:T(1,128)S(1)}, u32[]{:S(2)}) copy-start(f32[1,1,512]{2,1,0:T(1,128)S(1)} %get-tuple-element.744) | copy-start | bytes 6148
  16.5 38.9 %copy-start.70 = (f32[1,1,512]{2,1,0:T(1,128)}, f32[1,1,512]{2,1,0:T(1,128)S(1)}, u32[]{:S(2)}) copy-start(f32[1,1,512]{2,1,0:T(1,128)S(1)} %get-tuple-element.743) | copy-start | bytes 6148
  16.5 38.9 %copy-start.72 = (f32[1,1,512]{2,1,0:T(1,128)}, f32[1,1,512]{2,1,0:T(1,128)S(1)}, u32[]{:S(2)}) copy-start(f32[1,1,512]{2,1,0:T(1,128)S(1)} %get-tuple-element.739) | copy-start | bytes 6148
  16.5 38.9 %copy-start.74 = (f32[1,1,512]{2,1,0:T(1,128)}, f32[1,1,512]{2,1,0:T(1,128)S(1)}, u32[]{:S(2)}) copy-start(f32[1,1,512]{2,1,0:T(1,128)S(1)} %get-tuple-element.740) | copy-start | bytes 6148
  47.0 8.4 copy-start.10
  47.0 8.4 copy-start.12
  63.7 6.7 copy-start.35
  64.7 6.7 copy-start.37
  64.8 8.7 copy-start.54
  64.8 8.7 copy-start.56
  122.7 29.8 %copy-start.4 = (bf16[64,2048]{1,0:T(8,128)(2,1)S(1)}, bf16[64,2048]{1,0:T(8,128)(2,1)}, u32[]{:S(2)}) copy-start(bf16[64,2048]{1,0:T(8,128)(2,1)} %param.16) | copy-start | bytes 786436
  122.7 31.0 %copy-start.45 = (f32[2048]{0:T(1024)S(1)}, f32[2048]{0:T(1024)}, u32[]{:S(2)}) copy-start(f32[2048]{0:T(1024)} %param.23) | copy-start | bytes 24580
  124.4 57.7 %all-gather.9.cloned.1.call-start = ((), (), s32[]{:S(2)}) async-start(), calls=%async_computation.6 | async-start | bytes 1310720 | tf_op jit(solution)/shard_map/all_gather | solution.py:149
  153.7 103.1 %copy-start.92 = (f32[64]{0:T(128)}, f32[64]{0:T(128)S(1)}, u32[]{:S(2)}) copy-start(f32[64]{0:T(128)S(1)} %fusion.139) | copy-start | bytes 772
  155.5 54.9 %all-gather.11.cloned.1.call-start = ((), (), s32[]{:S(2)}) async-start(), calls=%async_computation.8 | async-start | bytes 1310720 | tf_op jit(solution)/shard_map/all_gather | solution.py:164
  156.1 98.8 %reduce-scatter.9.cloned.1.call-start = ((), (), s32[]{:S(2)}) async-start(), calls=%async_computation.9 | async-start | bytes 1310720 | tf_op jit(solution)/shard_map/reduce_scatter | solution.py:174
  226.8 58.7 %all-gather.13.cloned.1.call-start = ((), (), s32[]{:S(2)}) async-start(), calls=%async_computation.10 | async-start | bytes 1310720 | tf_op jit(solution)/shard_map/all_gather | solution.py:184
  258.8 236.8 %reduce-scatter.11.cloned.1.call-start = ((), (), s32[]{:S(2)}) async-start(), calls=%async_computation.11 | async-start | bytes 1310720 | tf_op jit(solution)/shard_map/reduce_scatter | solution.py:199
  430.9 104.7 %reduce-scatter.7.cloned.1.call-start = ((), (), s32[]{:S(2)}) async-start(), calls=%async_computation.7 | async-start | bytes 1310720 | tf_op jit(solution)/shard_map/reduce_scatter | solution.py:157
  436.7 440.3 %all-reduce.43.cloned.1.call-start = ((), (), s32[]{:S(2)}) async-start(), calls=%async_computation.13 | async-start | bytes 38797312 | tf_op jit(solution)/shard_map/psum | solution.py:219
  442.5 6.4 copy-start.26
  442.5 6.4 copy-start.28
  451.0 855.1 %all-gather.15.cloned.1.call-start = ((), (), s32[]{:S(2)}) async-start(), calls=%async_computation.12 | async-start | bytes 56623104 | tf_op jit(solution)/shard_map/all_gather | solution.py:213
  465.5 30.0 %copy-start.90 = (f32[512]{0:T(512)S(1)}, f32[512]{0:T(512)}, u32[]{:S(2)}) copy-start(f32[512]{0:T(512)} %get-tuple-element.769) | copy-start | bytes 6148
  465.5 30.1 %copy-start.46 = (f32[2048]{0:T(1024)S(1)}, f32[2048]{0:T(1024)}, u32[]{:S(2)}) copy-start(f32[2048]{0:T(1024)} %param.17) | copy-start | bytes 24580
  465.5 30.1 %copy-start.96 = (f32[64]{0:T(128)S(1)}, f32[64]{0:T(128)}, u32[]{:S(2)}) copy-start(f32[64]{0:T(128)} %copy-done.95) | copy-start | bytes 772
  465.5 31.4 %copy-start.58 = (f32[2048]{0:T(1024)S(1)}, f32[2048]{0:T(1024)}, u32[]{:S(2)}) copy-start(f32[2048]{0:T(1024)} %get-tuple-element.620) | copy-start | bytes 24580
  465.5 70.1 %copy-start.100 = (f32[64]{0:T(128)S(1)}, f32[64]{0:T(128)}, u32[]{:S(2)}) copy-start(f32[64]{0:T(128)} %copy-done.99) | copy-start | bytes 772
  465.5 70.1 %copy-start.6 = (bf16[64,2048]{1,0:T(8,128)(2,1)S(1)}, bf16[64,2048]{1,0:T(8,128)(2,1)}, u32[]{:S(2)}) copy-start(bf16[64,2048]{1,0:T(8,128)(2,1)} %reduce-scatter.5.cloned.1.call-done) | copy-start | bytes 786436
  465.5 70.1 %copy-start.31 = (bf16[64,2048]{1,0:T(8,128)(2,1)S(1)}, bf16[64,2048]{1,0:T(8,128)(2,1)}, u32[]{:S(2)}) copy-start(bf16[64,2048]{1,0:T(8,128)(2,1)} %param.27) | copy-start | bytes 786436
  465.5 70.1 %copy-start.32 = (bf16[64,2048]{1,0:T(8,128)(2,1)S(1)}, bf16[64,2048]{1,0:T(8,128)(2,1)}, u32[]{:S(2)}) copy-start(bf16[64,2048]{1,0:T(8,128)(2,1)} %reduce-scatter.9.cloned.1.call-done) | copy-start | bytes 786436
  465.6 70.1 %copy-start.93 = (f32[64]{0:T(128)S(1)}, f32[64]{0:T(128)}, u32[]{:S(2)}) copy-start(f32[64]{0:T(128)} %copy-done.92) | copy-start | bytes 772
  465.6 70.1 %copy-start.98 = (f32[64]{0:T(128)S(1)}, f32[64]{0:T(128)}, u32[]{:S(2)}) copy-start(f32[64]{0:T(128)} %copy-done.97) | copy-start | bytes 772
  1334.9 9.6 copy-start.1
  (72 other events, 171.2 us)
Sparse Core Ops, SparseCore 0:
  11.5 29.2 all-gather.6
  124.5 27.9 reduce-scatter.4
  155.6 26.4 all-gather.8
  183.8 26.4 all-gather.10
  226.9 27.9 reduce-scatter.8
  258.9 26.4 all-gather.12
  431.0 27.9 reduce-scatter.10
  461.9 27.9 reduce-scatter.6
  493.8 383.1 all-reduce.42
  878.5 427.4 all-gather.14
